TPU v7x, 32 devices: a whole 2x2x4 slice. The times are simulated.
32 devices in a mesh: req: 4 (over y, x), seq: 8 (over z, core).
Axes of the slice: x: 2, y: 2, z: 4, core: 2. Of those that a mesh axis runs over, the one named last changes fastest.
Arguments:
- residual: bfloat16 [64, 2048], P(None, ('req', 'seq')), may hold values from -90 to 90
- query_plain: bfloat16 [64, 16, 128], P('req'), may hold values from -6 to 6
- query_rotary: bfloat16 [64, 16, 64], P('req'), may hold values from -110 to 110
- latent_cache: bfloat16 [64, 3072, 512], P('req', 'seq'), may hold values from -9 to 9
- rotary_cache: bfloat16 [64, 64, 3072], P('req', None, 'seq'), may hold values from -4.5 to 4.5
- lengths: int32 [64], P('req'), may hold values from 2 to 3072, as said below
- absorb_key: bfloat16 [16, 128, 512], replicated, may hold values from -0.5 to 0.5
- absorb_value: bfloat16 [16, 512, 128], replicated, may hold values from -0.25 to 0.25
- output_weight: bfloat16 [2048, 2048], P(None, ('req', 'seq')), may hold values from -0.125 to 0.125
- middle_gain: float32 [2048], replicated, may hold values from 0.5 to 1.5
- routes: int32 [64, 6], replicated, may hold values from 0 to 63, all different within a row
- route_weights: float32 [64, 6], replicated, may hold values from 0.05 to 0.45
- gate_weight: bfloat16 [64, 2048, 1408], P('seq', None, 'req'), may hold values from -0.125 to 0.125
- up_weight: bfloat16 [64, 2048, 1408], P('seq', None, 'req'), may hold values from -0.125 to 0.125
- down_weight: bfloat16 [64, 1408, 2048], P('seq', 'req'), may hold values from -0.15625 to 0.15625
- shared_gate: bfloat16 [2048, 2816], P(None, ('req', 'seq')), may hold values from -0.125 to 0.125
- shared_up: bfloat16 [2048, 2816], P(None, ('req', 'seq')), may hold values from -0.125 to 0.125
- shared_down: bfloat16 [2816, 2048], P(('req', 'seq')), may hold values from -0.109375 to 0.109375
- final_gain: float32 [2048], replicated, may hold values from 0.5 to 1.5
- unembed: bfloat16 [102400, 2048], P(('req', 'seq')), may hold values from -0.65115609 to 0.65115609
Outputs:
- layer_out: bfloat16 [64, 2048], P(None, ('req', 'seq'))
- best_logits: float32 [64, 2], replicated
Inputs may be any that keep to these rules, and one draw needn't show every extreme that they name: Request r uses cache positions 0 to lengths[r] - 1, the new token's entry included; in every draw some request's cache is full.
All inputs are finite; a program needn't handle non-finite values.
Results may differ from a plain program's by a relative error of at most 0.0095.
Values may be sent and summed in bfloat16 or wider, within the bound.
A program may use at most 128 MiB of HBM per device.

v0:
```python
import jax
import jax.numpy as jnp
from jax import lax
from jax.sharding import PartitionSpec as P

NEG_FILL = -1e30
NORM_EPS = 1e-06


def combined_all(x, axis, join):
    gathered = jax.tree.map(
        lambda a, kind: lax.all_gather(a.astype(kind), axis),
        x,
        (jnp.bfloat16, jnp.bfloat16, jnp.bfloat16),
    )

    def take(source):
        return jax.tree.map(
            lambda a, own: lax.dynamic_index_in_dim(a, source, 0, False).astype(own.dtype),
            gathered,
            x,
        )

    return lax.fori_loop(
        1, lax.axis_size(axis), lambda source, state: join(state, take(source)), take(0)
    )


def merged_2(x, axis, combine):
    everything = lax.all_gather(x, axis)
    first = everything[0]

    def hop(k, so_far):
        return combine(so_far, everything[k])

    return lax.fori_loop(1, lax.axis_size(axis), hop, first)


def normed(hidden, gain):
    widened = hidden.astype(jnp.float32)
    meansq = jnp.mean(widened * widened, axis=-1, keepdims=True)
    return (widened * lax.rsqrt(meansq + NORM_EPS) * gain).astype(jnp.bfloat16)


def blend(former, latter):
    largest = jnp.maximum(former[0], latter[0])
    former_rescale = jnp.exp(former[0] - largest)
    latter_rescale = jnp.exp(latter[0] - largest)
    totals = former_rescale * former[1] + latter_rescale * latter[1]
    mixes = former_rescale[..., None] * former[2] + latter_rescale[..., None] * latter[2]
    return (largest, totals, mixes)


def best_two(former, latter):
    higher = jnp.maximum(former[:, 0], latter[:, 0])
    lower = jnp.maximum(
        jnp.minimum(former[:, 0], latter[:, 0]), jnp.maximum(former[:, 1], latter[:, 1])
    )
    return jnp.stack([higher, lower], axis=1)


def local(
    residual,
    query_plain,
    query_rotary,
    latent_cache,
    rotary_cache,
    lengths,
    absorb_key,
    absorb_value,
    output_weight,
    middle_gain,
    routes,
    route_weights,
    gate_weight,
    up_weight,
    down_weight,
    shared_gate,
    shared_up,
    shared_down,
    final_gain,
    unembed,
):
    group_rows, head_count, plain_size = query_plain.shape
    block_len = latent_cache.shape[1]
    value_size = absorb_value.shape[2]
    score_scale = (plain_size + query_rotary.shape[2]) ** (-0.5)
    value_wide = absorb_value.astype(jnp.float32)
    query_latent = jnp.einsum(
        "rhn,hnc->rhc", query_plain, absorb_key, preferred_element_type=jnp.float32
    ).astype(jnp.bfloat16)
    scores = jnp.einsum(
        "rhc,rtc->rht", query_latent, latent_cache, preferred_element_type=jnp.float32
    )
    scores = (
        scores
        + jnp.einsum("rhj,rjt->rht", query_rotary, rotary_cache, preferred_element_type=jnp.float32)
    ) * score_scale
    position = lax.axis_index("seq") * block_len + lax.broadcasted_iota(
        jnp.int32, (1, 1, block_len), 2
    )
    usable = position < lengths[:, None, None]
    block_peak = jnp.max(jnp.where(usable, scores, NEG_FILL), axis=2)
    weights = jnp.where(usable, jnp.exp(scores - block_peak[:, :, None]), 0.0).astype(jnp.bfloat16)
    block_total = jnp.sum(weights.astype(jnp.float32), axis=2)
    block_mix = jnp.einsum(
        "rht,rtc->rhc", weights, latent_cache, preferred_element_type=jnp.float32
    )
    merged_peak, merged_total, merged_mix = combined_all(
        (block_peak, block_total, block_mix), "seq", blend
    )
    merged = merged_mix / merged_total[:, :, None]
    merged = jnp.einsum("rhc,hcv->rhv", merged, value_wide, precision=lax.Precision.HIGHEST)
    group_output = merged.astype(jnp.bfloat16).reshape(group_rows, head_count * value_size)
    attn_out = jnp.dot(
        lax.all_gather(group_output, "req", axis=0, tiled=True),
        output_weight,
        preferred_element_type=jnp.float32,
    )
    column_count = residual.shape[1]
    stream_cols = (residual.astype(jnp.float32) + attn_out).astype(jnp.bfloat16)
    stream = lax.all_gather(stream_cols, ("req", "seq"), axis=1, tiled=True)
    expert_in = normed(stream, middle_gain)
    local_count = gate_weight.shape[0]
    expert_index = lax.axis_index("seq") * local_count + lax.broadcasted_iota(
        jnp.int32, (local_count, 1, 1), 0
    )
    route_share = jnp.sum(
        jnp.where(routes[None, :, :] == expert_index, route_weights[None, :, :], 0.0), axis=2
    )
    gate = jnp.einsum("td,edf->etf", expert_in, gate_weight, preferred_element_type=jnp.float32)
    upper = jnp.einsum("td,edf->etf", expert_in, up_weight, preferred_element_type=jnp.float32)
    expert_act = (jax.nn.silu(gate) * upper).astype(jnp.bfloat16)
    expert_back = jnp.einsum(
        "etf,efd->etd", expert_act, down_weight, preferred_element_type=jnp.float32
    )
    shared_gated = jnp.dot(expert_in, shared_gate, preferred_element_type=jnp.float32)
    shared_upper = jnp.dot(expert_in, shared_up, preferred_element_type=jnp.float32)
    shared_act = (jax.nn.silu(shared_gated) * shared_upper).astype(jnp.bfloat16)
    shared_back = jnp.dot(shared_act, shared_down, preferred_element_type=jnp.float32)
    expert_term = jnp.sum(route_share[:, :, None] * expert_back, axis=0) + shared_back
    column_start = lax.axis_index(("req", "seq")) * column_count
    moe = lax.psum(expert_term, ("req", "seq"))
    layer_full = (stream.astype(jnp.float32) + moe).astype(jnp.bfloat16)
    layer_out = lax.dynamic_slice_in_dim(layer_full, column_start, column_count, 1)
    final_in = normed(layer_full, final_gain)
    logits = lax.dot_general(
        final_in, unembed, (((1,), (1,)), ((), ())), preferred_element_type=jnp.float32
    )
    local_best = lax.top_k(logits, 2)[0]
    best_logits = merged_2(local_best, ("req", "seq"), best_two)
    return (layer_out, best_logits)


def solution(mesh):
    in_specs = (
        P(None, ("req", "seq")),
        P("req", None, None),
        P("req", None, None),
        P("req", "seq", None),
        P("req", None, "seq"),
        P("req"),
        P(),
        P(),
        P(None, ("req", "seq")),
        P(),
        P(),
        P(),
        P("seq", None, "req"),
        P("seq", None, "req"),
        P("seq", "req", None),
        P(None, ("req", "seq")),
        P(None, ("req", "seq")),
        P(("req", "seq"), None),
        P(),
        P(("req", "seq"), None),
    )
    out_specs = (P(None, ("req", "seq")), P())
    return jax.shard_map(local, mesh=mesh, in_specs=in_specs, out_specs=out_specs, check_vma=False)
```

profile of v0, /device:TPU:0, one launch (start us, length us, event | category | flops | bytes accessed | tf_op | source)
XLA Modules:
  0.0 327.6 jit_solution(13177338711063554684)
XLA Ops:
  7.2 0.0 copy-start
  7.2 0.0 all-gather.7.cloned.1.call-start
  7.3 0.0 copy-start.2
  7.3 0.9 broadcast_compare_fusion
  8.2 0.6 copy-done
  8.8 1.9 fusion.6
  10.7 4.5 %fusion.24 = f32[16,16,384]{2,1,0:T(8,128)S(1)} fusion(bf16[16,384,512]{2,1,0:T(8,128)(2,1)} %param.27, bf16[16,16,512]{2,0,1:T(8,128)(2,1)S(1)} %fusion.6), kind=kOutput, calls=%fused_computation.49 | convolution fusion | flops 100663296 | bytes 6946816 | tf_op jit(solution)/shard_map/rhc,rtc->rht/dot_general | solution.py:92
  15.3 0.0 copy-start.12
  15.3 0.3 select_reduce_fusion
  15.6 1.7 convolution_convert_fusion.1
  17.3 0.0 all-gather.7.cloned.1.call-update
  17.4 0.0 all-reduce.2.cloned.1.call-start
  17.5 0.2 fusion.34
  17.7 15.8 %all-gather.1 = bf16[128,16]{1,0:T(8,128)(2,1)S(1)} all-gather(bf16[16,16]{1,0:T(8,128)(2,1)S(1)} %fusion.34), channel_id=3, replica_groups=mesh['req'=4,'seq'=8] {'seq'}, dimensions={0}, use_global_device_ids=true | all-gather | bytes 4608 | tf_op jit(solution)/shard_map/all_gather | solution.py:12
  33.5 14.1 %all-gather = bf16[128,16]{1,0:T(8,128)(2,1)S(1)} all-gather(bf16[16,16]{1,0:T(8,128)(2,1)S(1)} %convert_element_type.122), channel_id=2, replica_groups=mesh['req'=4,'seq'=8] {'seq'}, dimensions={0}, use_global_device_ids=true | all-gather | bytes 4608 | tf_op jit(solution)/shard_map/all_gather | solution.py:12
  47.6 0.1 select_reduce_fusion.1
  47.7 2.0 all-gather.7.cloned.1.call-done
  49.6 1.0 slice_convert_fusion
  50.6 8.3 %while.34 = (s32[]{:T(128)}, f32[16,16]{1,0:T(8,128)S(1)}, f32[16,16]{1,0:T(8,128)S(1)}, f32[16,16,512]{2,1,0:T(8,128)S(1)}, bf16[8,16,16]{2,1,0:T(8,128)(2,1)S(...) while((s32[]{:T(128)}, f32[16,16]{1,0:T(8,128)S(1)}, ...), condition=%wide.region_3.4_spmd, body=%wide.region_2.3_spmd.sunk | while | flops 526341 | bytes 1320087 | solution.py:24
  50.7 1.2 fusion.66
  51.9 1.1 fusion.66
  53.1 1.1 fusion.66
  54.3 1.1 fusion.66
  55.4 1.1 fusion.66
  56.6 1.1 fusion.66
  57.8 1.1 fusion.66
  58.9 0.1 broadcast_divide_fusion
  59.0 2.8 fusion.7
  61.8 8.9 %all_gather.33 = bf16[64,2048]{1,0:T(8,128)(2,1)S(1)} all-gather(bf16[16,2048]{1,0:T(8,128)(2,1)S(1)} %bitcast.66), channel_id=1, replica_groups=mesh['req'=4,'seq'=8] {'req'}, dimensions={0}, use_global_device_ids=true | all-gather | bytes 327680 | tf_op jit(solution)/shard_map/all_gather | solution.py:116
  70.8 0.2 fusion.9
  71.0 0.1 copy.44
  71.1 41.6 %all_gather.34 = bf16[64,2048]{0,1:T(8,128)(2,1)S(1)} all-gather(bf16[64,64]{0,1:T(8,128)(2,1)S(1)} %copy.44), channel_id=1, replica_groups=mesh['req'=4,'seq'=8] {'req','seq'}, dimensions={1}, use_global_device_ids=true | all-gather | bytes 270336 | tf_op jit(solution)/shard_map/all_gather | solution.py:122
  112.7 0.2 copy.45
  112.9 0.2 fusion.13
  113.1 0.3 fusion.41
  113.4 7.9 %convolution_bitcast_fusion.1 = f32[8,64,352]{2,1,0:T(8,128)S(1)} fusion(bf16[8,2048,352]{1,2,0:T(8,128)(2,1)} %param.36, bf16[64,2048]{1,0:T(8,128)(2,1)S(1)} %copy.45, f32[2048]{0:T(1024)S(1)} %copy-done.7, f32[64]{0:T(128)S(1)} %add_rsqrt_fusion.1), kind=kOutput, calls=%fused_computation.15 | convolution fusion | flops 738721792 | bytes 12525824 | tf_op jit(solution)/shard_map/td,edf->etf/dot_general | solution.py:131
  121.4 13.4 %multiply_reduce_fusion = f32[64,2048]{1,0:T(8,128)S(1)} fusion(bf16[8,352,2048]{2,1,0:T(8,128)(2,1)} %param.38, f32[8,64]{1,0:T(8,128)S(1)} %select_reduce_fusion.1, bf16[8,2048,352]{1,2,0:T(8,128)(2,1)} %param.37, f32[8,64,352]{2,1,0:T(8,128)S(1)} %convolution_bitcast_fusion.1, bf16[64,2048]{1,0:T(8,128)(2,1)S(1)} %copy.45, f32[2048]{0:T(1024)S(1)} %copy-done.7, ...), kind=kOutput, calls=%fused_computation.12 | convolution fusion | flops 1479966720 | bytes 24586496 | tf_op jit(solution)/shard_map/etf,efd->etd/dot_general | solution.py:134
  134.8 1.4 convolution_add_fusion
  136.2 0.0 all-reduce.2.cloned.1.call-update
  136.3 125.3 %all-reduce.2.cloned.1.call-done = f32[64,2048]{1,0:T(8,128)} async-done(((f32[64,2048]{1,0:T(8,128)}), f32[64,2048]{1,0:T(8,128)}) %all-reduce.2.cloned.1.call-update) | async-done | bytes 524304 | tf_op jit(solution)/shard_map/psum | solution.py:143
  261.6 1.2 fusion.10
  262.8 9.0 %fusion.19 = f32[64,3200]{1,0:T(8,128)S(1)} fusion(bf16[3200,2048]{1,0:T(8,128)(2,1)} %param.43, bf16[64,2048]{1,0:T(8,128)(2,1)S(1)} %get-tuple-element.299, f32[2048]{0:T(1024)S(1)} %copy-done.11, f32[64]{0:T(128)S(1)} %add_rsqrt_fusion), kind=kOutput, calls=%fused_computation.45 | convolution fusion | flops 839385088 | bytes 14196992 | tf_op jit(solution)/shard_map/dot_general | solution.py:147
  271.8 6.6 %top_k.7 = (f32[64,2]{1,0:T(8,128)S(1)}, s32[64,2]{1,0:T(8,128)}) custom-call(f32[64,3200]{1,0:T(8,128)S(1)} %fusion.19), custom_call_target="TopK", called_computations={%compare_greater_than.1.10.clone.clone} | custom-call | tf_op jit(solution)/shard_map/top_k | solution.py:150
  278.4 0.1 copy.46
  278.4 39.6 %all-gather.4 = f32[32,64,2]{1,2,0:T(2,128)S(1)} all-gather(f32[1,64,2]{1,2,0:T(2,128)S(1)} %bitcast.69), channel_id=5, replica_groups=mesh['req'=4,'seq'=8] {'req','seq'}, dimensions={0}, use_global_device_ids=true | all-gather | bytes 16896 | tf_op jit(solution)/shard_map/all_gather | solution.py:30
  318.0 2.0 while.35
  320.0 0.0 copy-start.9
  320.0 0.7 constant_dynamic-slice_fusion
  (134 shorter events, 1.0 us)
Async XLA Ops:
  7.2 1.6 copy-start
  7.2 8.1 %copy-start.8 = (bf16[16,16,64]{2,1,0:T(8,128)(2,1)S(1)}, bf16[16,16,64]{2,1,0:T(8,128)(2,1)}, u32[]{:S(2)}) copy-start(bf16[16,16,64]{2,1,0:T(8,128)(2,1)} %param.26) | copy-start | bytes 98308
  7.2 8.1 %copy-start.3 = (bf16[16,64,384]{2,1,0:T(8,128)(2,1)S(1)}, bf16[16,64,384]{2,1,0:T(8,128)(2,1)}, u32[]{:S(2)}) copy-start(bf16[16,64,384]{2,1,0:T(8,128)(2,1)} %param.28) | copy-start | bytes 2359300
  7.2 42.4 %all-gather.7.cloned.1.call-start = ((), (), s32[]{:S(2)}) async-start(), calls=%async_computation.1 | async-start | bytes 2359296 | tf_op jit(solution)/shard_map/all_gather | solution.py:12
  7.3 8.4 %copy-start.2 = (bf16[16,384,512]{2,1,0:T(8,128)(2,1)S(1)}, bf16[16,384,512]{2,1,0:T(8,128)(2,1)}, u32[]{:S(2)}) copy-start(bf16[16,384,512]{2,1,0:T(8,128)(2,1)} %param.27) | copy-start | bytes 18874372
  15.3 32.3 %copy-start.12 = (f32[64,6]{0,1:T(8,128)S(1)}, f32[64,6]{0,1:T(8,128)}, u32[]{:S(2)}) copy-start(f32[64,6]{0,1:T(8,128)} %param.35) | copy-start | bytes 4612
  15.3 32.3 %copy-start.13 = (s32[64,6]{0,1:T(8,128)S(1)}, s32[64,6]{0,1:T(8,128)}, u32[]{:S(2)}) copy-start(s32[64,6]{0,1:T(8,128)} %param.34) | copy-start | bytes 4612
  17.4 244.2 %all-reduce.2.cloned.1.call-start = ((), (), s32[]{:S(2)}) async-start(), calls=%async_computation | async-start | bytes 1048576 | tf_op jit(solution)/shard_map/psum | solution.py:143
  17.4 53.4 %copy-start.6 = (bf16[2048,64]{0,1:T(8,128)(2,1)S(1)}, bf16[2048,64]{0,1:T(8,128)(2,1)}, u32[]{:S(2)}) copy-start(bf16[2048,64]{0,1:T(8,128)(2,1)} %param.32) | copy-start | bytes 786436
  17.4 53.3 %copy-start.10 = (bf16[64,64]{1,0:T(8,128)(2,1)S(1)}, bf16[64,64]{1,0:T(8,128)(2,1)}, u32[]{:S(2)}) copy-start(bf16[64,64]{1,0:T(8,128)(2,1)} %param.24) | copy-start | bytes 24580
  50.6 62.5 %copy-start.7 = (f32[2048]{0:T(1024)S(1)}, f32[2048]{0:T(1024)}, u32[]{:S(2)}) copy-start(f32[2048]{0:T(1024)} %param.33) | copy-start | bytes 24580
  50.6 62.5 %copy-start.14 = (bf16[2048,88]{0,1:T(8,128)(2,1)S(1)}, bf16[2048,88]{0,1:T(8,128)(2,1)}, u32[]{:S(2)}) copy-start(bf16[2048,88]{0,1:T(8,128)(2,1)} %param.39) | copy-start | bytes 1081348
  121.4 13.4 %copy-start.4 = (bf16[88,2048]{1,0:T(8,128)(2,1)S(1)}, bf16[88,2048]{1,0:T(8,128)(2,1)}, u32[]{:S(2)}) copy-start(bf16[88,2048]{1,0:T(8,128)(2,1)} %param.41) | copy-start | bytes 1081348
  121.4 13.4 %copy-start.5 = (bf16[2048,88]{0,1:T(8,128)(2,1)S(1)}, bf16[2048,88]{0,1:T(8,128)(2,1)}, u32[]{:S(2)}) copy-start(bf16[2048,88]{0,1:T(8,128)(2,1)} %param.40) | copy-start | bytes 1081348
  121.4 141.4 %copy-start.11 = (f32[2048]{0:T(1024)S(1)}, f32[2048]{0:T(1024)}, u32[]{:S(2)}) copy-start(f32[2048]{0:T(1024)} %param.42) | copy-start | bytes 24580
  262.8 57.9 %copy-start.1 = (bf16[16,128,512]{2,1,0:T(8,128)(2,1)S(1)}, bf16[16,128,512]{2,1,0:T(8,128)(2,1)}, u32[]{:S(2)}) copy-start(bf16[16,128,512]{2,1,0:T(8,128)(2,1)} %param.30) | copy-start | bytes 6291460
  320.0 0.7 copy-start.9
Sparse Core Ops, SparseCore 0:
  17.5 32.0 all-gather.6
  136.4 125.1 all-reduce.1
where the time goes:
time: 328 us
  waiting for transfers between devices  127 us (39%)
  blocking collectives  120 us (37%)
  matrix products  43.5 us (13%)
  other arithmetic  18.8 us (6%)
  between operations  14.4 us (4%)
    psum x1, waiting for transfers between devices, local(): moe = lax.psum(expert_term, ('req', 'seq'))  125 us
    all_gather x1, blocking collectives, local(): stream = lax.all_gather(stream_cols, ('req', 'seq'), axis=1, tiled=True)  41.6 us
    all_gather x1, blocking collectives, merged_2(): everything = lax.all_gather(x, axis)  39.6 us
    all_gather x2, blocking collectives, combined_all(): lax.all_gather(a.astype(kind), axis)  29.9 us
    dot_general x1, matrix products, local(): jnp.einsum('etf,efd->etd', expert_act, down_weight, preferred_element_typ...  13.4 us
    dot_general x1, matrix products, local(): lax.dot_general(final_in, unembed, (((1,), (1,)), ((), ())), preferred_el...  8.97 us
    all_gather x1, blocking collectives, local(): lax.all_gather(group_output, 'req', axis=0, tiled=True)  8.95 us
    dot_general x1, matrix products, local(): jnp.einsum('td,edf->etf', expert_in, gate_weight, preferred_element_type=...  7.94 us
  transfers between devices with their start and end apart: 2, of which 2 were waited for; matrix products, arithmetic and copies ran while one was open for 0% of the time, Pallas kernels for 0%

commit v1 on v0

--- a/solution.py
+++ b/solution.py
@@ -1,6 +1,9 @@
+import functools
 import jax
 import jax.numpy as jnp
 from jax import lax
+from jax.experimental import pallas as pl
+from jax.experimental.pallas import tpu as pltpu
 from jax.sharding import PartitionSpec as P
 
 NEG_FILL = -1e30
@@ -152,6 +155,649 @@
     return (layer_out, best_logits)
 
 
+NT = (((1,), (1,)), ((), ()))
+SLOTS = 4
+VOCAB_PIECES = 5
+MESH = pl.DeviceIdType.MESH
+
+
+def layer_kernel(
+    n_req,
+    n_seq,
+    plain_size,
+    lengths_ref,
+    query_latent_ref,
+    query_rotary_ref,
+    residual_ref,
+    routes_ref,
+    route_weights_ref,
+    middle_gain_ref,
+    final_gain_ref,
+    latent_hbm,
+    rotary_hbm,
+    value_hbm,
+    output_hbm,
+    gate_hbm,
+    up_hbm,
+    down_hbm,
+    shared_gate_hbm,
+    shared_up_hbm,
+    shared_down_hbm,
+    unembed_hbm,
+    layer_ref,
+    best_ref,
+    latent_buf,
+    rotary_buf,
+    value_buf,
+    output_buf,
+    residual_buf,
+    gate_buf,
+    up_buf,
+    down_buf,
+    shared_gate_buf,
+    shared_up_buf,
+    shared_down_buf,
+    unembed_buf,
+    stage,
+    mix_send,
+    mix_recv,
+    heads_send,
+    heads_full,
+    stream_full,
+    normed_buf,
+    moe_acc,
+    moe_send,
+    moe_recv,
+    layer_full,
+    best_send,
+    best_recv,
+    latent_sem,
+    local_sem,
+    expert_sem,
+    unembed_sem,
+    pair_sem,
+    mix_sem,
+    heads_sem,
+    stream_sem,
+    moe_sem,
+    layer_sem,
+    best_sem,
+):
+    n_dev = n_req * n_seq
+    n_pair = n_dev // 2
+    rows, heads, latent = query_latent_ref.shape
+    block_len = latent_hbm.shape[1]
+    experts = gate_hbm.shape[0]
+    tokens, width = stream_full.shape
+    half = tokens // 2
+    own_heads = heads // n_seq
+    mix_rows = own_heads * rows
+    chunks = latent // 128
+    score_scale = (plain_size + query_rotary_ref.shape[2]) ** (-0.5)
+    req = lax.axis_index("req")
+    seq = lax.axis_index("seq")
+    me = req * n_seq + seq
+    core = lax.rem(seq, 2)
+    pair = lax.div(me, 2)
+
+    def place(d):
+        return (lax.div(d, n_seq), lax.rem(d, n_seq))
+
+    barrier = pltpu.get_barrier_semaphore()
+
+    @pl.loop(1, n_dev)
+    def _(k):
+        pl.semaphore_signal(
+            barrier, inc=1, device_id=place(lax.rem(me + k, n_dev)), device_id_type=MESH
+        )
+
+    def latent_copy(i):
+        slot = lax.rem(i, SLOTS)
+        return pltpu.make_async_copy(latent_hbm.at[i], latent_buf.at[slot], latent_sem.at[slot])
+
+    my_output_rows = pl.ds(pl.multiple_of(core * 64, 64), 64)
+    local_copies = [
+        pltpu.make_async_copy(rotary_hbm, rotary_buf, local_sem.at[0]),
+        pltpu.make_async_copy(
+            value_hbm.at[pl.ds(seq * own_heads, own_heads)], value_buf, local_sem.at[1]
+        ),
+        pltpu.make_async_copy(output_hbm, output_buf.at[my_output_rows], local_sem.at[2]),
+        pltpu.make_async_copy(shared_gate_hbm, shared_gate_buf, local_sem.at[3]),
+        pltpu.make_async_copy(shared_up_hbm, shared_up_buf, local_sem.at[4]),
+        pltpu.make_async_copy(shared_down_hbm, shared_down_buf, local_sem.at[5]),
+    ]
+
+    def expert_copy(which, e):
+        source, target = ((gate_hbm, gate_buf), (up_hbm, up_buf), (down_hbm, down_buf))[which]
+        return pltpu.make_async_copy(source.at[e], target.at[e], expert_sem.at[which, e])
+
+    piece = unembed_hbm.shape[0] // VOCAB_PIECES
+
+    def unembed_copy(v):
+        place_rows = pl.ds(pl.multiple_of(v * piece, 64), piece)
+        return pltpu.make_async_copy(
+            unembed_hbm.at[place_rows], unembed_buf.at[place_rows], unembed_sem.at[v]
+        )
+
+    local_copies[0].start()
+    for i in range(SLOTS):
+        latent_copy(i).start()
+    for copy in local_copies[1:]:
+        copy.start()
+    local_copies[0].wait()
+    residual_buf[core] = residual_ref[...]
+
+    lane = lax.broadcasted_iota(jnp.int32, (heads, 128), 1)
+    position = seq * block_len + lax.broadcasted_iota(jnp.int32, (heads, block_len), 1)
+
+    @pl.loop(0, rows)
+    def _(i):
+        slot = lax.rem(i, SLOTS)
+        latent_copy(i).wait()
+        cached = latent_buf[slot]
+        scores = lax.dot_general(
+            query_latent_ref[i], cached, NT, preferred_element_type=jnp.float32
+        )
+        scores = (
+            scores
+            + jnp.dot(query_rotary_ref[i], rotary_buf[i], preferred_element_type=jnp.float32)
+        ) * score_scale
+        usable = position < lengths_ref[i]
+        peak = jnp.max(jnp.where(usable, scores, NEG_FILL), axis=1, keepdims=True)
+        weights = jnp.where(usable, jnp.exp(scores - peak), 0.0).astype(jnp.bfloat16)
+        total = jnp.sum(weights.astype(jnp.float32), axis=1, keepdims=True)
+        mix = jnp.dot(weights, cached, preferred_element_type=jnp.float32)
+        for c in range(chunks):
+            stage[c, pl.ds(i, heads, stride=rows), :] = mix[:, c * 128 : (c + 1) * 128]
+        info = jnp.zeros((heads, 128), jnp.float32)
+        at = 0
+        for value in (peak, total):
+            rest = value
+            for _ in range(3):
+                part = rest.astype(jnp.bfloat16).astype(jnp.float32)
+                info = jnp.where(lane == at, part, info)
+                rest = rest - part
+                at += 1
+        stage[chunks, pl.ds(i, heads, stride=rows), :] = info
+
+        @pl.when(i + SLOTS < rows)
+        def _():
+            latent_copy(i + SLOTS).start()
+
+        @pl.when(i < experts)
+        def _():
+            expert_copy(0, i).start()
+            expert_copy(1, i).start()
+            expert_copy(2, i).start()
+
+    for v in range(VOCAB_PIECES):
+        unembed_copy(v).start()
+
+    pl.semaphore_wait(barrier, n_dev - 1)
+
+    def mix_copy(k):
+        other = lax.rem(seq + k, n_seq)
+        source = lax.rem(seq + n_seq - k, n_seq)
+        sent = pltpu.make_async_remote_copy(
+            src_ref=mix_send.at[other],
+            dst_ref=mix_recv.at[seq],
+            send_sem=mix_sem.at[0, k],
+            recv_sem=mix_sem.at[1, seq],
+            device_id=(req, other),
+            device_id_type=MESH,
+        )
+        got = pltpu.make_async_remote_copy(
+            src_ref=mix_send.at[other],
+            dst_ref=mix_recv.at[source],
+            send_sem=mix_sem.at[0, k],
+            recv_sem=mix_sem.at[1, source],
+            device_id=(req, other),
+            device_id_type=MESH,
+        )
+        return sent, got
+
+    @pl.loop(1, n_seq)
+    def _(k):
+        other = lax.rem(seq + k, n_seq)
+        mine = pl.ds(pl.multiple_of(other * mix_rows, 16), mix_rows)
+        mix_send[other] = stage[:, mine, :].astype(jnp.bfloat16)
+        mix_copy(k)[0].start()
+
+    mix_recv[seq] = stage[:, pl.ds(pl.multiple_of(seq * mix_rows, 16), mix_rows), :].astype(
+        jnp.bfloat16
+    )
+
+    sibling = (req, seq + 1 - 2 * core)
+    their_output_rows = pl.ds(pl.multiple_of((1 - core) * 64, 64), 64)
+
+    def pair_copies(to_rows, to_slot):
+        return (
+            pltpu.make_async_remote_copy(
+                src_ref=output_hbm,
+                dst_ref=output_buf.at[to_rows],
+                send_sem=pair_sem.at[0],
+                recv_sem=pair_sem.at[1],
+                device_id=sibling,
+                device_id_type=MESH,
+            ),
+            pltpu.make_async_remote_copy(
+                src_ref=residual_buf.at[core],
+                dst_ref=residual_buf.at[to_slot],
+                send_sem=pair_sem.at[2],
+                recv_sem=pair_sem.at[3],
+                device_id=sibling,
+                device_id_type=MESH,
+            ),
+        )
+
+    pair_sends = pair_copies(my_output_rows, core)
+    pair_gets = pair_copies(their_output_rows, 1 - core)
+    for copy in pair_sends:
+        copy.start()
+
+    @pl.loop(1, n_seq)
+    def _(k):
+        mix_copy(k)[1].wait_recv()
+
+    info = mix_recv[:, chunks].astype(jnp.float32)
+    info_lane = lax.broadcasted_iota(jnp.int32, info.shape, 2)
+    peaks = jnp.sum(jnp.where(info_lane < 3, info, 0.0), axis=2, keepdims=True)
+    totals = jnp.sum(
+        jnp.where(info_lane < 3, 0.0, info), axis=2, keepdims=True
+    )
+    rescale = jnp.exp(peaks - jnp.max(peaks, axis=0, keepdims=True))
+    denominator = jnp.sum(rescale * totals, axis=0)
+    local_copies[1].wait()
+    attended = jnp.concatenate(
+        [
+            jnp.sum(rescale * mix_recv[:, c].astype(jnp.float32), axis=0) / denominator
+            for c in range(chunks)
+        ],
+        axis=1,
+    )
+    upper_part = attended.astype(jnp.bfloat16)
+    lower_part = (attended - upper_part.astype(jnp.float32)).astype(jnp.bfloat16)
+    value_size = value_buf.shape[2]
+    for j in range(own_heads):
+        span = slice(j * rows, (j + 1) * rows)
+        made = jnp.dot(upper_part[span], value_buf[j], preferred_element_type=jnp.float32)
+        made += jnp.dot(lower_part[span], value_buf[j], preferred_element_type=jnp.float32)
+        heads_send[:, j * value_size : (j + 1) * value_size] = made.astype(jnp.bfloat16)
+
+    head_cols = own_heads * value_size
+    wanted_core = lax.div(req, n_req // 2)
+    in_half = n_req // 2
+
+    def heads_slot(r, s):
+        return heads_full.at[
+            pl.ds(pl.multiple_of(lax.rem(r, in_half) * rows, rows), rows),
+            pl.ds(pl.multiple_of(s * head_cols, 128), head_cols),
+        ]
+
+    def heads_copy(target, r, s):
+        return pltpu.make_async_remote_copy(
+            src_ref=heads_send,
+            dst_ref=heads_slot(r, s),
+            send_sem=heads_sem.at[0, lax.div(target, 2)],
+            recv_sem=heads_sem.at[1, lax.rem(r, in_half) * n_seq + s],
+            device_id=place(target),
+            device_id_type=MESH,
+        )
+
+    @pl.loop(0, n_pair)
+    def _(k):
+        target = lax.rem(pair + 1 + k, n_pair) * 2 + wanted_core
+
+        @pl.when(target != me)
+        def _():
+            heads_copy(target, req, seq).start()
+
+    @pl.when(core == wanted_core)
+    def _():
+        heads_slot(req, seq)[...] = heads_send[...]
+
+    for copy in pair_gets:
+        copy.wait_recv()
+    local_copies[2].wait()
+
+    @pl.loop(0, n_pair)
+    def _(k):
+        r = core * in_half + lax.div(k, n_seq)
+        s = lax.rem(k, n_seq)
+
+        @pl.when(r * n_seq + s != me)
+        def _():
+            heads_copy(core, r, s).wait_recv()
+
+    my_rows = pl.ds(pl.multiple_of(core * half, half), half)
+    my_cols = pl.ds(pl.multiple_of(pair * 128, 128), 128)
+    attn_out = lax.dot_general(
+        heads_full[...], output_buf[...], NT, preferred_element_type=jnp.float32
+    )
+    entering = jnp.concatenate(
+        [residual_buf[0, my_rows, :], residual_buf[1, my_rows, :]], axis=1
+    ).astype(jnp.float32)
+    stream_full[my_rows, my_cols] = (entering + attn_out).astype(jnp.bfloat16)
+
+    def block_of(ref, d):
+        return ref.at[
+            pl.ds(pl.multiple_of(lax.rem(d, 2) * half, half), half),
+            pl.ds(pl.multiple_of(lax.div(d, 2) * 128, 128), 128),
+        ]
+
+    def spread_copy(ref, sem, k, owner):
+        return pltpu.make_async_remote_copy(
+            src_ref=block_of(ref, owner),
+            dst_ref=block_of(ref, owner),
+            send_sem=sem.at[0, k],
+            recv_sem=sem.at[1, owner],
+            device_id=place(lax.rem(me + k, n_dev)),
+            device_id_type=MESH,
+        )
+
+    def spread(ref, sem):
+        @pl.loop(1, n_dev)
+        def _(k):
+            spread_copy(ref, sem, k, me).start()
+
+    def collect(ref, sem):
+        @pl.loop(1, n_dev)
+        def _(k):
+            spread_copy(ref, sem, k, lax.rem(me + n_dev - k, n_dev)).wait_recv()
+
+    spread(stream_full, stream_sem)
+    for copy in local_copies[3:]:
+        copy.wait()
+    collect(stream_full, stream_sem)
+    normed_buf[...] = normed(stream_full[...], middle_gain_ref[...])
+
+    def glu(gate_rows, up_rows):
+        hidden = normed_buf[...]
+        gate = lax.dot_general(hidden, gate_rows, NT, preferred_element_type=jnp.float32)
+        upper = lax.dot_general(hidden, up_rows, NT, preferred_element_type=jnp.float32)
+        return (gate / (1.0 + jnp.exp(-gate)) * upper).astype(jnp.bfloat16)
+
+    spans = [slice(c * 512, (c + 1) * 512) for c in range(width // 512)]
+    shared_act = glu(shared_gate_buf[...], shared_up_buf[...])
+    for span in spans:
+        moe_acc[:, span] = jnp.dot(
+            shared_act, shared_down_buf[:, span], preferred_element_type=jnp.float32
+        )
+
+    @pl.loop(0, experts)
+    def _(e):
+        for which in range(3):
+            expert_copy(which, e).wait()
+        share = jnp.sum(
+            jnp.where(routes_ref[...] == seq * experts + e, route_weights_ref[...], 0.0),
+            axis=1,
+            keepdims=True,
+        )
+        act = glu(gate_buf[e], up_buf[e])
+        for span in spans:
+            moe_acc[:, span] += share * jnp.dot(
+                act, down_buf[e, :, span], preferred_element_type=jnp.float32
+            )
+
+    moe_send[...] = moe_acc[...].astype(jnp.bfloat16)
+
+    def moe_copy(k, owner):
+        target = lax.rem(me + k, n_dev)
+        return pltpu.make_async_remote_copy(
+            src_ref=block_of(moe_send, target),
+            dst_ref=moe_recv.at[owner],
+            send_sem=moe_sem.at[0, k],
+            recv_sem=moe_sem.at[1, owner],
+            device_id=place(target),
+            device_id_type=MESH,
+        )
+
+    @pl.loop(1, n_dev)
+    def _(k):
+        moe_copy(k, me).start()
+
+    moe_recv[me] = moe_send[my_rows, my_cols]
+
+    @pl.loop(1, n_dev)
+    def _(k):
+        moe_copy(k, lax.rem(me + n_dev - k, n_dev)).wait_recv()
+
+    moe = jnp.sum(moe_recv[...].astype(jnp.float32), axis=0)
+    layer_full[my_rows, my_cols] = (
+        stream_full[my_rows, my_cols].astype(jnp.float32) + moe
+    ).astype(jnp.bfloat16)
+    spread(layer_full, layer_sem)
+    collect(layer_full, layer_sem)
+    shown = layer_full[:, my_cols].astype(jnp.float32)
+    layer_ref[...] = jnp.where(core == 0, shown[:, :64], shown[:, 64:]).astype(jnp.bfloat16)
+    normed_buf[...] = normed(layer_full[...], final_gain_ref[...])
+
+    lowest = jnp.full((tokens, 128), -jnp.inf, jnp.float32)
+
+    def vocab_step(v, state):
+        first, second = state
+        unembed_copy(v).wait()
+        logits = lax.dot_general(
+            normed_buf[...],
+            unembed_buf[pl.ds(pl.multiple_of(v * piece, 64), piece), :],
+            NT,
+            preferred_element_type=jnp.float32,
+        )
+        for c in range(piece // 128):
+            part = logits[:, c * 128 : (c + 1) * 128]
+            second = jnp.maximum(second, jnp.minimum(first, part))
+            first = jnp.maximum(first, part)
+        return first, second
+
+    first, second = lax.fori_loop(0, VOCAB_PIECES, vocab_step, (lowest, lowest))
+    token_lane = lax.broadcasted_iota(jnp.int32, (tokens, 128), 1)
+    top = jnp.max(first, axis=1, keepdims=True)
+    where_top = jnp.min(
+        jnp.where(first == top, token_lane, 128), axis=1, keepdims=True
+    )
+    runner = jnp.max(
+        jnp.where(token_lane == where_top, second, first), axis=1, keepdims=True
+    )
+    packed = jnp.where(token_lane == 0, top, runner)
+    packed = jnp.concatenate([packed, packed], axis=0).T
+    best_send[...] = packed[:8]
+    best_recv[me] = packed[:8]
+
+    def best_copy(k, owner):
+        return pltpu.make_async_remote_copy(
+            src_ref=best_send,
+            dst_ref=best_recv.at[owner],
+            send_sem=best_sem.at[0, k],
+            recv_sem=best_sem.at[1, owner],
+            device_id=place(lax.rem(me + k, n_dev)),
+            device_id_type=MESH,
+        )
+
+    @pl.loop(1, n_dev)
+    def _(k):
+        best_copy(k, me).start()
+
+    for copy in pair_sends:
+        copy.wait_send()
+
+    @pl.loop(1, n_seq)
+    def _(k):
+        mix_copy(k)[0].wait_send()
+
+    @pl.loop(0, n_pair)
+    def _(k):
+        target = k * 2 + wanted_core
+
+        @pl.when(target != me)
+        def _():
+            heads_copy(target, req, seq).wait_send()
+
+    @pl.loop(1, n_dev)
+    def _(k):
+        spread_copy(stream_full, stream_sem, k, me).wait_send()
+        moe_copy(k, me).wait_send()
+        spread_copy(layer_full, layer_sem, k, me).wait_send()
+
+    @pl.loop(1, n_dev)
+    def _(k):
+        best_copy(k, lax.rem(me + n_dev - k, n_dev)).wait_recv()
+
+    found = [best_recv[d] for d in range(n_dev)]
+    pairs = [(x[0:1], x[1:2]) for x in found]
+    while len(pairs) > 1:
+        joined = [
+            (
+                jnp.maximum(a[0], b[0]),
+                jnp.maximum(jnp.minimum(a[0], b[0]), jnp.maximum(a[1], b[1])),
+            )
+            for a, b in zip(pairs[0::2], pairs[1::2])
+        ]
+        pairs = joined
+    best_ref[0:1, :] = pairs[0][0][:, :tokens]
+    best_ref[1:2, :] = pairs[0][1][:, :tokens]
+
+    @pl.loop(1, n_dev)
+    def _(k):
+        best_copy(k, me).wait_send()
+
+
+def fits(n_req, n_seq, shapes):
+    residual, query, cache, unembed = shapes
+    return (
+        n_req % 2 == 0
+        and n_seq % 2 == 0
+        and query[1] % n_seq == 0
+        and query[0] % 16 == 0
+        and residual[1] == 64
+        and residual[0] == 64
+        and cache[1] % 128 == 0
+        and unembed[0] % (128 * VOCAB_PIECES) == 0
+        and n_req * n_seq & (n_req * n_seq - 1) == 0
+    )
+
+
+def fused(
+    n_req,
+    n_seq,
+    residual,
+    query_plain,
+    query_rotary,
+    latent_cache,
+    rotary_cache,
+    lengths,
+    absorb_key,
+    absorb_value,
+    output_weight,
+    middle_gain,
+    routes,
+    route_weights,
+    gate_weight,
+    up_weight,
+    down_weight,
+    shared_gate,
+    shared_up,
+    shared_down,
+    final_gain,
+    unembed,
+):
+    query_latent = jnp.einsum(
+        "rhn,hnc->rhc", query_plain, absorb_key, preferred_element_type=jnp.float32
+    ).astype(jnp.bfloat16)
+    rows, heads, latent = query_latent.shape
+    tokens = residual.shape[0]
+    width = unembed.shape[1]
+    n_dev = n_req * n_seq
+    block_len = latent_cache.shape[1]
+    experts, ff = gate_weight.shape[0], gate_weight.shape[2]
+    shared_ff = shared_gate.shape[1]
+    own_heads = heads // n_seq
+    value_size = absorb_value.shape[2]
+    parts = latent // 128 + 1
+    bf, f32 = jnp.bfloat16, jnp.float32
+    dma = pltpu.SemaphoreType.DMA
+    vmem = pl.BlockSpec(memory_space=pltpu.VMEM)
+    anywhere = pl.BlockSpec(memory_space=pl.ANY)
+    layer_out, best = pl.pallas_call(
+        functools.partial(layer_kernel, n_req, n_seq, query_plain.shape[2]),
+        name="layer",
+        out_shape=(
+            jax.ShapeDtypeStruct(residual.shape, bf),
+            jax.ShapeDtypeStruct((2, tokens), f32),
+        ),
+        in_specs=[pl.BlockSpec(memory_space=pltpu.SMEM)] + [vmem] * 7 + [anywhere] * 11,
+        out_specs=(vmem, vmem),
+        scratch_shapes=[
+            pltpu.VMEM((SLOTS, block_len, latent), bf),
+            pltpu.VMEM(rotary_cache.shape, bf),
+            pltpu.VMEM((own_heads, latent, value_size), bf),
+            pltpu.VMEM((128, width), bf),
+            pltpu.VMEM((2, tokens, 64), bf),
+            pltpu.VMEM((experts, ff, width), bf),
+            pltpu.VMEM((experts, ff, width), bf),
+            pltpu.VMEM((experts, ff, width), bf),
+            pltpu.VMEM((shared_ff, width), bf),
+            pltpu.VMEM((shared_ff, width), bf),
+            pltpu.VMEM((shared_ff, width), bf),
+            pltpu.VMEM(unembed.shape, bf),
+            pltpu.VMEM((parts, heads * rows, 128), f32),
+            pltpu.VMEM((n_seq, parts, own_heads * rows, 128), bf),
+            pltpu.VMEM((n_seq, parts, own_heads * rows, 128), bf),
+            pltpu.VMEM((rows, own_heads * value_size), bf),
+            pltpu.VMEM((tokens // 2, heads * value_size), bf),
+            pltpu.VMEM((tokens, width), bf),
+            pltpu.VMEM((tokens, width), bf),
+            pltpu.VMEM((tokens, width), f32),
+            pltpu.VMEM((tokens, width), bf),
+            pltpu.VMEM((n_dev, tokens // 2, 128), bf),
+            pltpu.VMEM((tokens, width), bf),
+            pltpu.VMEM((8, 128), f32),
+            pltpu.VMEM((n_dev, 8, 128), f32),
+            dma((SLOTS,)),
+            dma((6,)),
+            dma((3, experts)),
+            dma((VOCAB_PIECES,)),
+            dma((4,)),
+            dma((2, n_seq)),
+            dma((2, n_dev // 2)),
+            dma((2, n_dev)),
+            dma((2, n_dev)),
+            dma((2, n_dev)),
+            dma((2, n_dev)),
+        ],
+        compiler_params=pltpu.CompilerParams(
+            collective_id=0, has_side_effects=True, vmem_limit_bytes=63 * 1024 * 1024
+        ),
+    )(
+        lengths,
+        query_latent,
+        query_rotary,
+        residual,
+        routes,
+        route_weights,
+        middle_gain.reshape(1, width),
+        final_gain.reshape(1, width),
+        latent_cache,
+        rotary_cache,
+        absorb_value,
+        output_weight.T,
+        jnp.swapaxes(gate_weight, 1, 2),
+        jnp.swapaxes(up_weight, 1, 2),
+        down_weight,
+        shared_gate.T,
+        shared_up.T,
+        shared_down,
+        unembed,
+    )
+    return layer_out, best.T
+
+
+def chosen(n_req, n_seq, *args):
+    shapes = (args[0].shape, args[1].shape, args[3].shape, args[19].shape)
+    if fits(n_req, n_seq, shapes):
+        return fused(n_req, n_seq, *args)
+    return local(*args)
+
+
 def solution(mesh):
     in_specs = (
         P(None, ("req", "seq")),
@@ -176,4 +822,5 @@
         P(("req", "seq"), None),
     )
     out_specs = (P(None, ("req", "seq")), P())
-    return jax.shard_map(local, mesh=mesh, in_specs=in_specs, out_specs=out_specs, check_vma=False)
+    body = functools.partial(chosen, mesh.shape["req"], mesh.shape["seq"])
+    return jax.shard_map(body, mesh=mesh, in_specs=in_specs, out_specs=out_specs, check_vma=False)

time: 328 us -> 92.7 us (0.28)
  waiting for transfers between devices: 127 us -> 0 us
  blocking collectives: 120 us -> 0 us
  Pallas kernels: 0 us -> 83.7 us
  matrix products: 43.5 us -> 2 us
  other arithmetic: 18.8 us -> 0 us
  between operations: 14.4 us -> 0.64 us
  local copies, waits for them, and re-layouts: 2.02 us -> 6.15 us
    psum x1 -> x0, waiting for transfers between devices: 125 us -> none  [local(): moe = lax.psum(expert_term, ('req', 'seq'))]
    all_gather x5 -> x0, blocking collectives: 120 us -> none  [the longest x1 41.6 us: local(): stream = lax.all_gather(stream_cols, ('req', 'seq'), axis=1, tiled=True)]
    pallas_call x0 -> x1, Pallas kernels: none -> 83.7 us  [fused(): pl.pallas_call(functools.partial(layer_kernel, n_req, n_seq, query_plain....]
    dot_general x11 -> x1, matrix products: 43.5 us -> 2 us  [fused(): jnp.einsum('rhn,hnc->rhc', query_plain, absorb_key, preferred_element_typ...]
    add x16 -> x0, other arithmetic: 8.04 us -> none  [the longest x7 7.89 us: blend(): former_rescale[..., None] * former[2]]
    top_k x1 -> x0, other arithmetic: 6.57 us -> none  [local(): local_best = lax.top_k(logits, 2)[0]]
    unnamed x30 -> x4, local copies, waits for them, and re-layouts: 0.73 us -> 5.29 us
  transfers between devices with their start and end apart: 2 -> 0, of which waited for: 2 -> 0; matrix products, arithmetic and copies ran while one was open for 0% -> 0% of each run, Pallas kernels for 0% -> 0%
where the time goes in v1:
time: 92.7 us; the launch traced here: 92.4 us
  Pallas kernels  83.7 us (90%)
  local copies, waits for them, and re-layouts  6.15 us (7%)
  matrix products  2 us (2%)
    pallas_call x1, Pallas kernels, fused(): pl.pallas_call(functools.partial(layer_kernel, n_req, n_seq, query_plain....  83.7 us
    unnamed x4, local copies, waits for them, and re-layouts  5.29 us
    dot_general x1, matrix products, fused(): jnp.einsum('rhn,hnc->rhc', query_plain, absorb_key, preferred_element_typ...  2 us

profile of v1, /device:TPU:0, one launch (start us, length us, event | category | flops | bytes accessed | tf_op | source)
XLA Modules:
  0.0 92.4 jit_solution(12852608980470315362)
XLA Ops:
  0.6 2.0 %fusion.1 = bf16[16,512,16]{1,2,0:T(8,128)(2,1)S(1)} fusion(bf16[16,128,512]{2,1,0:T(8,128)(2,1)} %param.26, bf16[16,16,128]{2,1,0:T(8,128)(2,1)} %param.21), kind=kOutput, calls=%fused_computation.2 | convolution fusion | flops 33554432 | bytes 2424832 | tf_op jit(solution)/shard_map/rhn,hnc->rhc/dot_general | solution.py:703
  2.6 0.9 copy.31
  3.5 1.4 %copy.24.routes_ref = s32[64,6]{1,0:T(8,128)} copy(s32[64,6]{0,1:T(8,128)} %param.30) | data formatting | bytes 3072 | tf_op args[10]
  4.9 1.4 %copy.25.route_weights_ref = f32[64,6]{1,0:T(8,128)} copy(f32[64,6]{0,1:T(8,128)} %param.31) | data formatting | bytes 3072 | tf_op args[11]
  6.3 83.7 %layer.1 = (bf16[64,64]{1,0:T(8,128)(2,1)}, f32[2,64]{1,0:T(2,128)}) custom-call(s32[16]{0:T(128)} %lengths_ref.1, bf16[16,16,512]{2,1,0:T(8,128)(2,1)} %bitcast.14, bf16[16,16,64]{2,1,0:T(8,128)(2,1)} %query_rotary_ref.1, bf16[64,64]{1,0:T(8,128)(2,1)} %residual_ref.1, s32[64,6]{1,0:T(8,128)} %copy.24.routes_ref, f32[64,6]{1,0:T(8,128)} %copy.25.route_weights_ref, ...), custom_call_target="tpu_custom_call" | custom-call | tf_op jit(solution)/shard_map/layer/pallas_call | solution.py:720
  89.9 1.3 %copy.34 = bf16[64,64]{1,0:T(8,128)(2,1)} copy(bf16[64,64]{1,0:T(8,128)(2,1)} %get-tuple-element.8) | data formatting | bytes 16384
  91.3 1.2 %copy.35 = f32[64,2]{0,1:T(2,128)} copy(f32[64,2]{0,1:T(2,128)} %bitcast.20) | data formatting | bytes 1024

commit v2 on v1

--- a/solution.py
+++ b/solution.py
@@ -207,9 +207,13 @@
     normed_buf,
     moe_acc,
     moe_send,
+    moe_theirs,
+    moe_sums,
     moe_recv,
     layer_full,
     best_send,
+    best_theirs,
+    best_sums,
     best_recv,
     latent_sem,
     local_sem,
@@ -479,31 +483,44 @@
     ).astype(jnp.float32)
     stream_full[my_rows, my_cols] = (entering + attn_out).astype(jnp.bfloat16)
 
-    def block_of(ref, d):
-        return ref.at[
-            pl.ds(pl.multiple_of(lax.rem(d, 2) * half, half), half),
-            pl.ds(pl.multiple_of(lax.div(d, 2) * 128, 128), 128),
-        ]
+    their_rows = pl.ds(pl.multiple_of((1 - core) * half, half), half)
+
+    def chip(p):
+        return place(lax.rem(p, n_pair) * 2 + core)
 
     def spread_copy(ref, sem, k, owner):
+        block = ref.at[my_rows, pl.ds(pl.multiple_of(owner * 128, 128), 128)]
         return pltpu.make_async_remote_copy(
-            src_ref=block_of(ref, owner),
-            dst_ref=block_of(ref, owner),
+            src_ref=block,
+            dst_ref=block,
             send_sem=sem.at[0, k],
             recv_sem=sem.at[1, owner],
-            device_id=place(lax.rem(me + k, n_dev)),
+            device_id=chip(pair + k),
             device_id_type=MESH,
         )
 
+    def half_copy(ref, sem, span):
+        return pltpu.make_async_remote_copy(
+            src_ref=ref.at[span],
+            dst_ref=ref.at[span],
+            send_sem=sem.at[0, 0],
+            recv_sem=sem.at[1, n_pair],
+            device_id=sibling,
+            device_id_type=MESH,
+        )
+
     def spread(ref, sem):
-        @pl.loop(1, n_dev)
+        @pl.loop(1, n_pair)
         def _(k):
-            spread_copy(ref, sem, k, me).start()
+            spread_copy(ref, sem, k, pair).start()
 
     def collect(ref, sem):
-        @pl.loop(1, n_dev)
+        @pl.loop(1, n_pair)
         def _(k):
-            spread_copy(ref, sem, k, lax.rem(me + n_dev - k, n_dev)).wait_recv()
+            spread_copy(ref, sem, k, lax.rem(pair + n_pair - k, n_pair)).wait_recv()
+
+        half_copy(ref, sem, my_rows).start()
+        half_copy(ref, sem, their_rows).wait_recv()
 
     spread(stream_full, stream_sem)
     for copy in local_copies[3:]:
@@ -539,28 +556,41 @@
                 act, down_buf[e, :, span], preferred_element_type=jnp.float32
             )
 
-    moe_send[...] = moe_acc[...].astype(jnp.bfloat16)
+    moe_send[...] = moe_acc[their_rows, :].astype(jnp.bfloat16)
+    moe_half = pltpu.make_async_remote_copy(
+        src_ref=moe_send,
+        dst_ref=moe_theirs,
+        send_sem=moe_sem.at[0, 0],
+        recv_sem=moe_sem.at[1, n_pair],
+        device_id=sibling,
+        device_id_type=MESH,
+    )
+    moe_half.start()
+    moe_half.wait_recv()
+    moe_sums[...] = (moe_acc[my_rows, :] + moe_theirs[...].astype(jnp.float32)).astype(
+        jnp.bfloat16
+    )
 
     def moe_copy(k, owner):
-        target = lax.rem(me + k, n_dev)
+        target = lax.rem(pair + k, n_pair)
         return pltpu.make_async_remote_copy(
-            src_ref=block_of(moe_send, target),
+            src_ref=moe_sums.at[:, pl.ds(pl.multiple_of(target * 128, 128), 128)],
             dst_ref=moe_recv.at[owner],
             send_sem=moe_sem.at[0, k],
             recv_sem=moe_sem.at[1, owner],
-            device_id=place(target),
+            device_id=chip(target),
             device_id_type=MESH,
         )
 
-    @pl.loop(1, n_dev)
-    def _(k):
-        moe_copy(k, me).start()
-
-    moe_recv[me] = moe_send[my_rows, my_cols]
-
-    @pl.loop(1, n_dev)
-    def _(k):
-        moe_copy(k, lax.rem(me + n_dev - k, n_dev)).wait_recv()
+    @pl.loop(1, n_pair)
+    def _(k):
+        moe_copy(k, pair).start()
+
+    moe_recv[pair] = moe_sums[:, my_cols]
+
+    @pl.loop(1, n_pair)
+    def _(k):
+        moe_copy(k, lax.rem(pair + n_pair - k, n_pair)).wait_recv()
 
     moe = jnp.sum(moe_recv[...].astype(jnp.float32), axis=0)
     layer_full[my_rows, my_cols] = (
@@ -601,21 +631,48 @@
     packed = jnp.where(token_lane == 0, top, runner)
     packed = jnp.concatenate([packed, packed], axis=0).T
     best_send[...] = packed[:8]
-    best_recv[me] = packed[:8]
+    best_half = pltpu.make_async_remote_copy(
+        src_ref=best_send,
+        dst_ref=best_theirs,
+        send_sem=best_sem.at[0, 0],
+        recv_sem=best_sem.at[1, n_pair],
+        device_id=sibling,
+        device_id_type=MESH,
+    )
+    best_half.start()
+    best_half.wait_recv()
+
+    def joined(a, b):
+        return (
+            jnp.maximum(a[0], b[0]),
+            jnp.maximum(jnp.minimum(a[0], b[0]), jnp.maximum(a[1], b[1])),
+        )
+
+    chip_best = joined(
+        (best_send[0:1, :], best_send[1:2, :]), (best_theirs[0:1, :], best_theirs[1:2, :])
+    )
+    best_sums[0:1, :] = chip_best[0]
+    best_sums[1:8, :] = jnp.broadcast_to(chip_best[1], (7, 128))
+    best_recv[pair] = best_sums[...]
 
     def best_copy(k, owner):
         return pltpu.make_async_remote_copy(
-            src_ref=best_send,
+            src_ref=best_sums,
             dst_ref=best_recv.at[owner],
             send_sem=best_sem.at[0, k],
             recv_sem=best_sem.at[1, owner],
-            device_id=place(lax.rem(me + k, n_dev)),
+            device_id=chip(pair + k),
             device_id_type=MESH,
         )
 
-    @pl.loop(1, n_dev)
-    def _(k):
-        best_copy(k, me).start()
+    @pl.loop(1, n_pair)
+    def _(k):
+        best_copy(k, pair).start()
+
+    moe_half.wait_send()
+    best_half.wait_send()
+    half_copy(stream_full, stream_sem, my_rows).wait_send()
+    half_copy(layer_full, layer_sem, my_rows).wait_send()
 
     for copy in pair_sends:
         copy.wait_send()
@@ -632,33 +689,26 @@
         def _():
             heads_copy(target, req, seq).wait_send()
 
-    @pl.loop(1, n_dev)
-    def _(k):
-        spread_copy(stream_full, stream_sem, k, me).wait_send()
-        moe_copy(k, me).wait_send()
-        spread_copy(layer_full, layer_sem, k, me).wait_send()
-
-    @pl.loop(1, n_dev)
-    def _(k):
-        best_copy(k, lax.rem(me + n_dev - k, n_dev)).wait_recv()
-
-    found = [best_recv[d] for d in range(n_dev)]
+    @pl.loop(1, n_pair)
+    def _(k):
+        spread_copy(stream_full, stream_sem, k, pair).wait_send()
+        moe_copy(k, pair).wait_send()
+        spread_copy(layer_full, layer_sem, k, pair).wait_send()
+
+    @pl.loop(1, n_pair)
+    def _(k):
+        best_copy(k, lax.rem(pair + n_pair - k, n_pair)).wait_recv()
+
+    found = [best_recv[d] for d in range(n_pair)]
     pairs = [(x[0:1], x[1:2]) for x in found]
     while len(pairs) > 1:
-        joined = [
-            (
-                jnp.maximum(a[0], b[0]),
-                jnp.maximum(jnp.minimum(a[0], b[0]), jnp.maximum(a[1], b[1])),
-            )
-            for a, b in zip(pairs[0::2], pairs[1::2])
-        ]
-        pairs = joined
+        pairs = [joined(a, b) for a, b in zip(pairs[0::2], pairs[1::2])]
     best_ref[0:1, :] = pairs[0][0][:, :tokens]
     best_ref[1:2, :] = pairs[0][1][:, :tokens]
 
-    @pl.loop(1, n_dev)
-    def _(k):
-        best_copy(k, me).wait_send()
+    @pl.loop(1, n_pair)
+    def _(k):
+        best_copy(k, pair).wait_send()
 
 
 def fits(n_req, n_seq, shapes):
@@ -747,11 +797,15 @@
             pltpu.VMEM((tokens, width), bf),
             pltpu.VMEM((tokens, width), bf),
             pltpu.VMEM((tokens, width), f32),
-            pltpu.VMEM((tokens, width), bf),
-            pltpu.VMEM((n_dev, tokens // 2, 128), bf),
+            pltpu.VMEM((tokens // 2, width), bf),
+            pltpu.VMEM((tokens // 2, width), bf),
+            pltpu.VMEM((tokens // 2, width), bf),
+            pltpu.VMEM((n_dev // 2, tokens // 2, 128), bf),
             pltpu.VMEM((tokens, width), bf),
             pltpu.VMEM((8, 128), f32),
-            pltpu.VMEM((n_dev, 8, 128), f32),
+            pltpu.VMEM((8, 128), f32),
+            pltpu.VMEM((8, 128), f32),
+            pltpu.VMEM((n_dev // 2, 8, 128), f32),
             dma((SLOTS,)),
             dma((6,)),
             dma((3, experts)),
@@ -759,10 +813,10 @@
             dma((4,)),
             dma((2, n_seq)),
             dma((2, n_dev // 2)),
-            dma((2, n_dev)),
-            dma((2, n_dev)),
-            dma((2, n_dev)),
-            dma((2, n_dev)),
+            dma((2, n_dev // 2 + 1)),
+            dma((2, n_dev // 2 + 1)),
+            dma((2, n_dev // 2 + 1)),
+            dma((2, n_dev // 2 + 1)),
         ],
         compiler_params=pltpu.CompilerParams(
             collective_id=0, has_side_effects=True, vmem_limit_bytes=63 * 1024 * 1024

time: 92.7 us -> 87.2 us (0.941)
  Pallas kernels: 83.7 us -> 78.1 us
    pallas_call x1, Pallas kernels: 83.7 us -> 78.1 us  [fused(): pl.pallas_call(functools.partial(layer_kernel, n_req, n_seq, query_plain....]
where the time goes in v2:
time: 87.2 us; the launch traced here: 86.9 us
  Pallas kernels  78.1 us (90%)
  local copies, waits for them, and re-layouts  6.15 us (7%)
  matrix products  2 us (2%)
    pallas_call x1, Pallas kernels, fused(): pl.pallas_call(functools.partial(layer_kernel, n_req, n_seq, query_plain....  78.1 us
    unnamed x4, local copies, waits for them, and re-layouts  5.29 us
    dot_general x1, matrix products, fused(): jnp.einsum('rhn,hnc->rhc', query_plain, absorb_key, preferred_element_typ...  2 us

profile of v2, /device:TPU:0, one launch (start us, length us, event | category | flops | bytes accessed | tf_op | source)
XLA Modules:
  0.0 86.9 jit_solution(16105003442986167609)
XLA Ops:
  0.6 2.0 %fusion.1 = bf16[16,512,16]{1,2,0:T(8,128)(2,1)S(1)} fusion(bf16[16,128,512]{2,1,0:T(8,128)(2,1)} %param.26, bf16[16,16,128]{2,1,0:T(8,128)(2,1)} %param.21), kind=kOutput, calls=%fused_computation.2 | convolution fusion | flops 33554432 | bytes 2424832 | tf_op jit(solution)/shard_map/rhn,hnc->rhc/dot_general | solution.py:753
  2.6 0.9 copy.31
  3.5 1.4 %copy.24.routes_ref = s32[64,6]{1,0:T(8,128)} copy(s32[64,6]{0,1:T(8,128)} %param.30) | data formatting | bytes 3072 | tf_op args[10]
  4.9 1.4 %copy.25.route_weights_ref = f32[64,6]{1,0:T(8,128)} copy(f32[64,6]{0,1:T(8,128)} %param.31) | data formatting | bytes 3072 | tf_op args[11]
  6.3 78.1 %layer.1 = (bf16[64,64]{1,0:T(8,128)(2,1)}, f32[2,64]{1,0:T(2,128)}) custom-call(s32[16]{0:T(128)} %lengths_ref.1, bf16[16,16,512]{2,1,0:T(8,128)(2,1)} %bitcast.14, bf16[16,16,64]{2,1,0:T(8,128)(2,1)} %query_rotary_ref.1, bf16[64,64]{1,0:T(8,128)(2,1)} %residual_ref.1, s32[64,6]{1,0:T(8,128)} %copy.24.routes_ref, f32[64,6]{1,0:T(8,128)} %copy.25.route_weights_ref, ...), custom_call_target="tpu_custom_call" | custom-call | tf_op jit(solution)/shard_map/layer/pallas_call | solution.py:770
  84.3 1.3 %copy.34 = bf16[64,64]{1,0:T(8,128)(2,1)} copy(bf16[64,64]{1,0:T(8,128)(2,1)} %get-tuple-element.8) | data formatting | bytes 16384
  85.7 1.2 %copy.35 = f32[64,2]{0,1:T(2,128)} copy(f32[64,2]{0,1:T(2,128)} %bitcast.20) | data formatting | bytes 1024

commit v3 on v2

--- a/solution.py
+++ b/solution.py
@@ -156,7 +156,6 @@
 
 
 NT = (((1,), (1,)), ((), ()))
-SLOTS = 4
 VOCAB_PIECES = 5
 MESH = pl.DeviceIdType.MESH
 
@@ -164,9 +163,8 @@
 def layer_kernel(
     n_req,
     n_seq,
-    plain_size,
     lengths_ref,
-    query_latent_ref,
+    query_plain_ref,
     query_rotary_ref,
     residual_ref,
     routes_ref,
@@ -175,6 +173,7 @@
     final_gain_ref,
     latent_hbm,
     rotary_hbm,
+    key_hbm,
     value_hbm,
     output_hbm,
     gate_hbm,
@@ -188,6 +187,9 @@
     best_ref,
     latent_buf,
     rotary_buf,
+    key_buf,
+    query_wide,
+    query_latent,
     value_buf,
     output_buf,
     residual_buf,
@@ -205,6 +207,7 @@
     heads_full,
     stream_full,
     normed_buf,
+    share_buf,
     moe_acc,
     moe_send,
     moe_theirs,
@@ -229,7 +232,8 @@
 ):
     n_dev = n_req * n_seq
     n_pair = n_dev // 2
-    rows, heads, latent = query_latent_ref.shape
+    rows, heads, plain_size = query_plain_ref.shape
+    latent = latent_hbm.shape[2]
     block_len = latent_hbm.shape[1]
     experts = gate_hbm.shape[0]
     tokens, width = stream_full.shape
@@ -256,8 +260,7 @@
         )
 
     def latent_copy(i):
-        slot = lax.rem(i, SLOTS)
-        return pltpu.make_async_copy(latent_hbm.at[i], latent_buf.at[slot], latent_sem.at[slot])
+        return pltpu.make_async_copy(latent_hbm.at[i], latent_buf.at[i], latent_sem.at[i])
 
     my_output_rows = pl.ds(pl.multiple_of(core * 64, 64), 64)
     local_copies = [
@@ -271,6 +274,8 @@
         pltpu.make_async_copy(shared_down_hbm, shared_down_buf, local_sem.at[5]),
     ]
 
+    key_copy = pltpu.make_async_copy(key_hbm, key_buf, local_sem.at[6])
+
     def expert_copy(which, e):
         source, target = ((gate_hbm, gate_buf), (up_hbm, up_buf), (down_hbm, down_buf))[which]
         return pltpu.make_async_copy(source.at[e], target.at[e], expert_sem.at[which, e])
@@ -283,24 +288,40 @@
             unembed_hbm.at[place_rows], unembed_buf.at[place_rows], unembed_sem.at[v]
         )
 
+    key_copy.start()
     local_copies[0].start()
-    for i in range(SLOTS):
+
+    @pl.loop(0, rows)
+    def _(i):
         latent_copy(i).start()
+
     for copy in local_copies[1:]:
         copy.start()
+    residual_buf[core] = residual_ref[...]
+    for r in range(rows):
+        query_wide[r * heads : (r + 1) * heads, :] = query_plain_ref[r].astype(jnp.float32)
+    key_copy.wait()
+    for h in range(heads):
+        made = jnp.dot(
+            query_wide[pl.ds(h, rows, stride=heads), :].astype(jnp.bfloat16),
+            key_buf[h],
+            preferred_element_type=jnp.float32,
+        )
+        for c in range(chunks):
+            query_latent[c, pl.ds(h, rows, stride=heads), :] = made[:, c * 128 : (c + 1) * 128]
     local_copies[0].wait()
-    residual_buf[core] = residual_ref[...]
 
     lane = lax.broadcasted_iota(jnp.int32, (heads, 128), 1)
     position = seq * block_len + lax.broadcasted_iota(jnp.int32, (heads, block_len), 1)
 
     @pl.loop(0, rows)
     def _(i):
-        slot = lax.rem(i, SLOTS)
         latent_copy(i).wait()
-        cached = latent_buf[slot]
+        cached = latent_buf[i]
+        here = pl.ds(pl.multiple_of(i * heads, heads), heads)
+        query = jnp.concatenate([query_latent[c, here, :] for c in range(chunks)], axis=1)
         scores = lax.dot_general(
-            query_latent_ref[i], cached, NT, preferred_element_type=jnp.float32
+            query.astype(jnp.bfloat16), cached, NT, preferred_element_type=jnp.float32
         )
         scores = (
             scores
@@ -324,10 +345,6 @@
                 at += 1
         stage[chunks, pl.ds(i, heads, stride=rows), :] = info
 
-        @pl.when(i + SLOTS < rows)
-        def _():
-            latent_copy(i + SLOTS).start()
-
         @pl.when(i < experts)
         def _():
             expert_copy(0, i).start()
@@ -399,6 +416,14 @@
     for copy in pair_sends:
         copy.start()
 
+    for e in range(experts):
+        share_row = jnp.sum(
+            jnp.where(routes_ref[...] == seq * experts + e, route_weights_ref[...], 0.0),
+            axis=0,
+            keepdims=True,
+        )
+        share_buf[e] = jnp.broadcast_to(share_row, (128, tokens)).T
+
     @pl.loop(1, n_seq)
     def _(k):
         mix_copy(k)[1].wait_recv()
@@ -545,11 +570,7 @@
     def _(e):
         for which in range(3):
             expert_copy(which, e).wait()
-        share = jnp.sum(
-            jnp.where(routes_ref[...] == seq * experts + e, route_weights_ref[...], 0.0),
-            axis=1,
-            keepdims=True,
-        )
+        share = jnp.concatenate([share_buf[e]] * 4, axis=1)
         act = glu(gate_buf[e], up_buf[e])
         for span in spans:
             moe_acc[:, span] += share * jnp.dot(
@@ -750,10 +771,8 @@
     final_gain,
     unembed,
 ):
-    query_latent = jnp.einsum(
-        "rhn,hnc->rhc", query_plain, absorb_key, preferred_element_type=jnp.float32
-    ).astype(jnp.bfloat16)
-    rows, heads, latent = query_latent.shape
+    rows, heads, plain_size = query_plain.shape
+    latent = latent_cache.shape[2]
     tokens = residual.shape[0]
     width = unembed.shape[1]
     n_dev = n_req * n_seq
@@ -768,17 +787,20 @@
     vmem = pl.BlockSpec(memory_space=pltpu.VMEM)
     anywhere = pl.BlockSpec(memory_space=pl.ANY)
     layer_out, best = pl.pallas_call(
-        functools.partial(layer_kernel, n_req, n_seq, query_plain.shape[2]),
+        functools.partial(layer_kernel, n_req, n_seq),
         name="layer",
         out_shape=(
             jax.ShapeDtypeStruct(residual.shape, bf),
             jax.ShapeDtypeStruct((2, tokens), f32),
         ),
-        in_specs=[pl.BlockSpec(memory_space=pltpu.SMEM)] + [vmem] * 7 + [anywhere] * 11,
+        in_specs=[pl.BlockSpec(memory_space=pltpu.SMEM)] + [vmem] * 7 + [anywhere] * 12,
         out_specs=(vmem, vmem),
         scratch_shapes=[
-            pltpu.VMEM((SLOTS, block_len, latent), bf),
+            pltpu.VMEM((rows, block_len, latent), bf),
             pltpu.VMEM(rotary_cache.shape, bf),
+            pltpu.VMEM(absorb_key.shape, bf),
+            pltpu.VMEM((rows * heads, plain_size), f32),
+            pltpu.VMEM((latent // 128, rows * heads, 128), f32),
             pltpu.VMEM((own_heads, latent, value_size), bf),
             pltpu.VMEM((128, width), bf),
             pltpu.VMEM((2, tokens, 64), bf),
@@ -796,6 +818,7 @@
             pltpu.VMEM((tokens // 2, heads * value_size), bf),
             pltpu.VMEM((tokens, width), bf),
             pltpu.VMEM((tokens, width), bf),
+            pltpu.VMEM((experts, tokens, 128), f32),
             pltpu.VMEM((tokens, width), f32),
             pltpu.VMEM((tokens // 2, width), bf),
             pltpu.VMEM((tokens // 2, width), bf),
@@ -806,8 +829,8 @@
             pltpu.VMEM((8, 128), f32),
             pltpu.VMEM((8, 128), f32),
             pltpu.VMEM((n_dev // 2, 8, 128), f32),
-            dma((SLOTS,)),
-            dma((6,)),
+            dma((rows,)),
+            dma((7,)),
             dma((3, experts)),
             dma((VOCAB_PIECES,)),
             dma((4,)),
@@ -823,15 +846,16 @@
         ),
     )(
         lengths,
-        query_latent,
+        query_plain,
         query_rotary,
         residual,
-        routes,
-        route_weights,
+        routes.T,
+        route_weights.T,
         middle_gain.reshape(1, width),
         final_gain.reshape(1, width),
         latent_cache,
         rotary_cache,
+        absorb_key,
         absorb_value,
         output_weight.T,
         jnp.swapaxes(gate_weight, 1, 2),

time: 87.2 us -> 76.2 us (0.87)
  Pallas kernels: 78.1 us -> 72.7 us
  local copies, waits for them, and re-layouts: 6.15 us -> 2.54 us
  matrix products: 2 us -> 0 us
    pallas_call x1, Pallas kernels: 78.1 us -> 72.7 us  [fused(): pl.pallas_call(functools.partial(layer_kernel, n_req, n_seq), name='layer...]
    unnamed x4 -> x2, local copies, waits for them, and re-layouts: 5.29 us -> 2.54 us
    dot_general x1 -> x0, matrix products: 2 us -> none  [fused(): jnp.einsum('rhn,hnc->rhc', query_plain, absorb_key, preferred_element_typ...]
where the time goes in v3:
time: 76.2 us; the launch traced here: 75.9 us
  Pallas kernels  72.7 us (95%)
  local copies, waits for them, and re-layouts  2.54 us (3%)
    pallas_call x1, Pallas kernels, fused(): pl.pallas_call(functools.partial(layer_kernel, n_req, n_seq), name='layer...  72.7 us
    unnamed x2, local copies, waits for them, and re-layouts  2.54 us

profile of v3, /device:TPU:0, one launch (start us, length us, event | category | flops | bytes accessed | tf_op | source)
XLA Modules:
  0.0 75.9 jit_solution(9815541650954248806)
XLA Ops:
  0.6 72.7 %layer.1 = (bf16[64,64]{1,0:T(8,128)(2,1)}, f32[2,64]{1,0:T(2,128)}) custom-call(s32[16]{0:T(128)} %lengths_ref.1, bf16[16,16,128]{2,1,0:T(8,128)(2,1)} %query_plain_ref.1, bf16[16,16,64]{2,1,0:T(8,128)(2,1)} %query_rotary_ref.1, bf16[64,64]{1,0:T(8,128)(2,1)} %residual_ref.1, s32[6,64]{1,0:T(8,128)} %bitcast.17, f32[6,64]{1,0:T(8,128)} %bitcast.18, ...), custom_call_target="tpu_custom_call" | custom-call | tf_op jit(solution)/shard_map/layer/pallas_call | solution.py:789
  73.4 1.3 %copy.24 = bf16[64,64]{1,0:T(8,128)(2,1)} copy(bf16[64,64]{1,0:T(8,128)(2,1)} %get-tuple-element.8) | data formatting | bytes 16384
  74.7 1.2 %copy.25 = f32[64,2]{0,1:T(2,128)} copy(f32[64,2]{0,1:T(2,128)} %bitcast.19) | data formatting | bytes 1024
